TPU v7x, 128 devices: a whole 4x4x4 slice. The times are simulated.
128 devices in a mesh: cent: 4 (over y), rows: 32 (over z, x, core).
Axes of the slice: x: 4, y: 4, z: 4, core: 2. Of those that a mesh axis runs over, the one named last changes fastest.
Arguments:
- embeddings: bfloat16 [32768, 2048], P(('cent', 'rows')), may hold values from -6 to 6
- centroids: bfloat16 [16384, 2048], P(('cent', 'rows')), may hold values from -0.125 to 0.125
- cluster: int32 [32768, 1], P(('cent', 'rows')), may hold values from 0 to 127; in each aligned block of 256 rows (0 to 255, 256 to 511, ...) at most 4 rows name the same one
- noise_salt: int32 [1], replicated, may hold values from 0 to 1048575
Outputs:
- perturbed_max: float32 [32768], P(('cent', 'rows'))
- dedup_score: float32 [32768], P(('cent', 'rows'))
- new_centroids: float32 [128, 2048], P(('cent', 'rows'))
Inputs may be any that keep to these rules, and one draw needn't show every extreme that they name: In every aligned block of 256 rows (the rows of one device) no cluster is named by more than 4 rows, and in some block some cluster by exactly 4; every cluster is named by some row.
All inputs are finite; a program needn't handle non-finite values.
Results may differ from a plain program's by a relative error of at most 0.0003.
Values may be sent and summed in bfloat16 or wider, within the bound.
A program may use at most 128 MiB of HBM per device.

v0:
```python
import math
import jax
import jax.numpy as jnp
from jax import lax
from jax.sharding import PartitionSpec as P

inverse_temp = 3.0
epsilon = 1e-06


def logical_shift(word, amount):
    return lax.shift_right_logical(word, jnp.full(word.shape, amount, jnp.int32))


def gumbel_noise(row_ids, cent_ids, salt_word):
    mixed = row_ids * 1103515245 + cent_ids * 739982445 + salt_word
    mixed = mixed ^ logical_shift(mixed, 16)
    mixed = mixed * 2146121005
    mixed = mixed ^ logical_shift(mixed, 15)
    mixed = mixed * 1759714725
    mixed = mixed ^ logical_shift(mixed, 16)
    low_bits = mixed & 8388607
    uniform = (low_bits.astype(jnp.float32) + 0.5) * (1.0 / 8388608.0)
    return -jnp.log(-jnp.log(uniform))


def cluster_stats(members, valid):
    feature_dim = members.shape[1]
    widened = members.astype(jnp.float32)
    scale = lax.rsqrt(jnp.mean(widened * widened, axis=1) + epsilon)
    gram = lax.dot_general(
        members, members, (((1,), (1,)), ((), ())), preferred_element_type=jnp.float32
    )
    similar = gram * scale[:, None] * scale[None, :] * (1.0 / math.sqrt(feature_dim))
    order = jnp.arange(members.shape[0], dtype=jnp.int32)
    usable = valid[None, :] & (order[:, None] != order[None, :])
    highest = jnp.max(jnp.where(usable, similar, -1e30), axis=1)
    scores = jnp.where(jnp.any(usable, axis=1), highest, 0.0)
    total = jnp.sum(jnp.where(valid[:, None], widened, 0.0), axis=0)
    center = total * lax.rsqrt(jnp.mean(total * total) + epsilon)
    return (scores, center)


def shards(embeddings, centroids, cluster, noise_salt):
    rows_dev, feature_dim = embeddings.shape
    cent_dev = centroids.shape[0]
    cent_count = lax.axis_size("cent")
    rows_count = lax.axis_size("rows")
    devices = cent_count * rows_count
    capacity = max(2, 2 * rows_dev // devices)
    cent_index = lax.axis_index("cent")
    rows_index = lax.axis_index("rows")
    salt_word = noise_salt[0]
    group = lax.all_gather(embeddings, "cent", axis=0, tiled=True)
    position = jnp.arange(cent_count * rows_dev, dtype=jnp.int32)
    group_ids = (position // rows_dev * rows_count + rows_index) * rows_dev + position % rows_dev
    panel_base = cent_index * (rows_count * cent_dev)
    initial = jnp.full((cent_count * rows_dev,), -1e30, jnp.float32)
    piece = lax.all_gather(centroids, "rows", axis=0, tiled=True)
    piece_rows = piece.shape[0]
    block = math.gcd(piece_rows, 512)
    tiles = piece.reshape(piece_rows // block, block, feature_dim)
    offsets = jnp.arange(piece_rows // block, dtype=jnp.int32) * block

    def step(carry, item):
        tile, offset = item
        scores = lax.dot_general(
            group, tile, (((1,), (1,)), ((), ())), preferred_element_type=jnp.float32
        )
        cent_ids = panel_base + offset + jnp.arange(block, dtype=jnp.int32)
        perturbed = inverse_temp * scores + gumbel_noise(
            group_ids[:, None], cent_ids[None, :], salt_word
        )
        return (jnp.maximum(carry, jnp.max(perturbed, axis=1)), None)

    result, unused = lax.scan(step, initial, (tiles, offsets))
    merged = lax.pmax(result, "cent")
    perturbed_max = lax.dynamic_slice_in_dim(merged, cent_index * rows_dev, rows_dev)
    assigned = cluster[:, 0]
    order = jnp.arange(rows_dev, dtype=jnp.int32)
    same = (assigned[:, None] == assigned[None, :]) & (order[None, :] < order[:, None])
    rank = jnp.sum(same.astype(jnp.int32), axis=1)
    slot = assigned * capacity + rank
    outgoing = jnp.zeros((devices * capacity, feature_dim), jnp.bfloat16).at[slot].set(embeddings)
    present = (
        jnp.zeros((devices * capacity,), jnp.bfloat16)
        .at[slot]
        .set(jnp.ones((rows_dev,), jnp.bfloat16))
    )
    received, arrived = (
        lax.all_to_all(
            outgoing.reshape(devices, capacity, feature_dim),
            ("cent", "rows"),
            split_axis=0,
            concat_axis=0,
            tiled=True,
        ),
        lax.all_to_all(
            present.reshape(devices, capacity),
            ("cent", "rows"),
            split_axis=0,
            concat_axis=0,
            tiled=True,
        ),
    )
    members = received.reshape(devices * capacity, feature_dim)
    valid = arrived.reshape(devices * capacity) > 0.5
    scores, center = cluster_stats(members, valid)
    returned = lax.all_to_all(
        scores.reshape(devices, capacity), ("cent", "rows"), split_axis=0, concat_axis=0, tiled=True
    )
    dedup_score = returned.reshape(devices * capacity)[slot]
    return (perturbed_max, dedup_score, center[None, :])


def solution(mesh):
    in_specs = (
        P(("cent", "rows"), None),
        P(("cent", "rows"), None),
        P(("cent", "rows"), None),
        P(),
    )
    out_specs = (P(("cent", "rows")), P(("cent", "rows")), P(("cent", "rows"), None))
    return jax.shard_map(shards, mesh=mesh, in_specs=in_specs, out_specs=out_specs, check_vma=False)
```

profile of v0, /device:TPU:0, one launch (start us, length us, event | category | flops | bytes accessed | tf_op | source)
XLA Modules:
  0.0 242.6 jit_solution(4939791693935059020)
XLA Ops:
  7.2 0.7 all-gather.5.cloned.1.call-update
  7.9 0.7 all-gather.3.cloned.1.call-update
  8.6 0.9 convert_reduce_fusion
  9.6 0.7 compare_select_fusion
  10.3 2.2 scatter_custom_fusion
  12.4 0.8 all_to_all.17
  13.2 11.1 %all-to-all-start = ((bf16[128,1,4]{2,1,0:T(2,128)(2,1)}), bf16[128,1,4]{2,1,0:T(2,128)(2,1)S(1)}, u32[]{:S(2)}, u32[]{:S(2)}) async-start(bf16[128,1,4]{2,1,0:T(2,128)(2,1)} %all_to_all.17), calls=%async_computation | async-start | bytes 131072 | tf_op jit(solution)/shard_map/all_to_all | solution.py:98
  24.3 3.5 %scatter_custom_fusion.1 = bf16[512,2048]{1,0:T(8,128)(2,1)S(1)} fusion(s32[256]{0:T(256)S(1)} %bitcast.32, bf16[256,2048]{1,0:T(8,128)(2,1)} %param.6, bf16[]{:T(256)} %constant.99.clone.1), kind=kCustom, calls=%fused_computation.50 | custom fusion | bytes 2097664 | tf_op jit(solution)/shard_map/scatter | solution.py:84
  27.9 2.2 reshape.113
  30.1 3.5 %all-to-all-done = bf16[128,1,4]{2,1,0:T(2,128)(2,1)S(1)} async-done(((bf16[128,1,4]{2,1,0:T(2,128)(2,1)}), bf16[128,1,4]{2,1,0:T(2,128)(2,1)S(1)}, u32[]{:S(2)}, u32[]{:S(2)}) %all-to-all-start) | async-done | bytes 1056 | tf_op jit(solution)/shard_map/all_to_all | solution.py:98
  33.6 6.3 %all-to-all-start.1 = ((bf16[128,4,2048]{2,1,0:T(4,128)(2,1)}), bf16[128,4,2048]{2,1,0:T(4,128)(2,1)S(1)}, u32[]{:S(2)}, u32[]{:S(2)}) async-start(bf16[128,4,2048]{2,1,0:T(4,128)(2,1)} %reshape.113), calls=%async_computation.1 | async-start | bytes 4194304 | tf_op jit(solution)/shard_map/all_to_all | solution.py:91
  40.7 32.1 %all-to-all-done.1 = bf16[128,4,2048]{2,1,0:T(4,128)(2,1)S(1)} async-done(((bf16[128,4,2048]{2,1,0:T(4,128)(2,1)}), bf16[128,4,2048]{2,1,0:T(4,128)(2,1)S(1)}, u32[]{:S(2)}, u32[]{:S(2)}) %all-to-all-start.1) | async-done | bytes 2097184 | tf_op jit(solution)/shard_map/all_to_all | solution.py:91
  72.8 2.1 fusion.33
  75.1 2.1 reshape.114
  77.1 3.6 %fusion.37 = f32[512]{0:T(512)S(1)} fusion(bf16[512,2048]{1,0:T(8,128)(2,1)} %reshape.114, f32[512]{0:T(512)S(1)} %rsqrt.18, pred[512]{0:T(512)(128)(4,1)S(1)} %gt.22), kind=kOutput, calls=%fused_computation.49 | convolution fusion | flops 1075576320 | bytes 2101760 | tf_op jit(solution)/shard_map/dot_general | solution.py:31
  80.7 0.7 select_n.51
  81.5 7.2 %all-to-all-start.2 = ((f32[128,1,4]{2,1,0:T(1,128)}), f32[128,1,4]{2,1,0:T(1,128)S(1)}, u32[]{:S(2)}, u32[]{:S(2)}) async-start(f32[128,1,4]{2,1,0:T(1,128)} %bitcast.5), calls=%async_computation.2 | async-start | bytes 131072 | tf_op jit(solution)/shard_map/all_to_all | solution.py:109
  90.6 7.2 %all-to-all-done.2 = f32[128,1,4]{2,1,0:T(1,128)S(1)} async-done(((f32[128,1,4]{2,1,0:T(1,128)}), f32[128,1,4]{2,1,0:T(1,128)S(1)}, u32[]{:S(2)}, u32[]{:S(2)}) %all-to-all-start.2) | async-done | bytes 2080 | tf_op jit(solution)/shard_map/all_to_all | solution.py:109
  98.3 0.8 reduce.7
  99.3 2.5 %gather_fusion = f32[256]{0:T(256)} fusion(f32[512]{0:T(512)S(1)} %reshape.115, s32[1024]{0:T(1024)S(1)} %pad_clamp_fusion), kind=kCustom, calls=%fused_computation | custom fusion | bytes 3072 | tf_op jit(solution)/shard_map/gather | solution.py:112
  101.8 57.1 %all-gather.3.cloned.1.call-done = bf16[4096,2048]{1,0:T(8,128)(2,1)} async-done(((bf16[128,2048]{1,0:T(8,128)(2,1)}), bf16[4096,2048]{1,0:T(8,128)(2,1)}) %all-gather.3.cloned.1.call-update) | async-done | bytes 16777232 | tf_op jit(solution)/shard_map/all_gather | solution.py:59
  158.8 65.8 %while.11 = (s32[]{:T(128)}, f32[1024]{0:T(1024)S(1)}, bf16[8,512,2048]{2,1,0:T(8,128)(2,1)}, bf16[1024,2048]{1,0:T(8,128)(2,1)}, s32[8]{0:T(128)S(1)}, /*index=...) while((s32[]{:T(128)}, f32[1024]{0:T(1024)S(1)}, bf16[8,512,2048]{2,1,0:T(8,128)(2,1)}, ...), condition=%wide.region_2.3_spmd.clone, body=%wide.region_0.2_spmd.clone.sunk | while | flops 2157464576 | bytes 6320795 | solution.py:76
  160.1 6.9 %fusion.56 = f32[1024]{0:T(1024)S(1)} fusion(bf16[1024,2048]{1,0:T(8,128)(2,1)} %get-tuple-element.168, bf16[8,512,2048]{2,1,0:T(8,128)(2,1)} %get-tuple-element.167, s32[]{:T(128)S(6)} %copy.19, s32[]{:T(128)} %get-tuple-element.171, s32[512]{0:T(512)S(1)} %add_multiply_fusion.2, s32[1024]{0:T(1024)S(1)} %fusion.55), kind=kOutput, calls=%fused_computation.21.clone.1 | convolution fusion | flops 2157444096 | bytes 6302212 | tf_op jit(solution)/shard_map/while/body/eval_jaxpr/dot_general | solution.py:67
  168.3 6.9 %fusion.56 = f32[1024]{0:T(1024)S(1)} fusion(bf16[1024,2048]{1,0:T(8,128)(2,1)} %get-tuple-element.168, bf16[8,512,2048]{2,1,0:T(8,128)(2,1)} %get-tuple-element.167, s32[]{:T(128)S(6)} %copy.19, s32[]{:T(128)} %get-tuple-element.171, s32[512]{0:T(512)S(1)} %add_multiply_fusion.2, s32[1024]{0:T(1024)S(1)} %fusion.55), kind=kOutput, calls=%fused_computation.21.clone.1 | convolution fusion | flops 2157444096 | bytes 6302212 | tf_op jit(solution)/shard_map/while/body/eval_jaxpr/dot_general | solution.py:67
  176.5 6.9 %fusion.56 = f32[1024]{0:T(1024)S(1)} fusion(bf16[1024,2048]{1,0:T(8,128)(2,1)} %get-tuple-element.168, bf16[8,512,2048]{2,1,0:T(8,128)(2,1)} %get-tuple-element.167, s32[]{:T(128)S(6)} %copy.19, s32[]{:T(128)} %get-tuple-element.171, s32[512]{0:T(512)S(1)} %add_multiply_fusion.2, s32[1024]{0:T(1024)S(1)} %fusion.55), kind=kOutput, calls=%fused_computation.21.clone.1 | convolution fusion | flops 2157444096 | bytes 6302212 | tf_op jit(solution)/shard_map/while/body/eval_jaxpr/dot_general | solution.py:67
  184.8 6.9 %fusion.56 = f32[1024]{0:T(1024)S(1)} fusion(bf16[1024,2048]{1,0:T(8,128)(2,1)} %get-tuple-element.168, bf16[8,512,2048]{2,1,0:T(8,128)(2,1)} %get-tuple-element.167, s32[]{:T(128)S(6)} %copy.19, s32[]{:T(128)} %get-tuple-element.171, s32[512]{0:T(512)S(1)} %add_multiply_fusion.2, s32[1024]{0:T(1024)S(1)} %fusion.55), kind=kOutput, calls=%fused_computation.21.clone.1 | convolution fusion | flops 2157444096 | bytes 6302212 | tf_op jit(solution)/shard_map/while/body/eval_jaxpr/dot_general | solution.py:67
  193.0 6.9 %fusion.56 = f32[1024]{0:T(1024)S(1)} fusion(bf16[1024,2048]{1,0:T(8,128)(2,1)} %get-tuple-element.168, bf16[8,512,2048]{2,1,0:T(8,128)(2,1)} %get-tuple-element.167, s32[]{:T(128)S(6)} %copy.19, s32[]{:T(128)} %get-tuple-element.171, s32[512]{0:T(512)S(1)} %add_multiply_fusion.2, s32[1024]{0:T(1024)S(1)} %fusion.55), kind=kOutput, calls=%fused_computation.21.clone.1 | convolution fusion | flops 2157444096 | bytes 6302212 | tf_op jit(solution)/shard_map/while/body/eval_jaxpr/dot_general | solution.py:67
  201.2 6.9 %fusion.56 = f32[1024]{0:T(1024)S(1)} fusion(bf16[1024,2048]{1,0:T(8,128)(2,1)} %get-tuple-element.168, bf16[8,512,2048]{2,1,0:T(8,128)(2,1)} %get-tuple-element.167, s32[]{:T(128)S(6)} %copy.19, s32[]{:T(128)} %get-tuple-element.171, s32[512]{0:T(512)S(1)} %add_multiply_fusion.2, s32[1024]{0:T(1024)S(1)} %fusion.55), kind=kOutput, calls=%fused_computation.21.clone.1 | convolution fusion | flops 2157444096 | bytes 6302212 | tf_op jit(solution)/shard_map/while/body/eval_jaxpr/dot_general | solution.py:67
  209.4 6.9 %fusion.56 = f32[1024]{0:T(1024)S(1)} fusion(bf16[1024,2048]{1,0:T(8,128)(2,1)} %get-tuple-element.168, bf16[8,512,2048]{2,1,0:T(8,128)(2,1)} %get-tuple-element.167, s32[]{:T(128)S(6)} %copy.19, s32[]{:T(128)} %get-tuple-element.171, s32[512]{0:T(512)S(1)} %add_multiply_fusion.2, s32[1024]{0:T(1024)S(1)} %fusion.55), kind=kOutput, calls=%fused_computation.21.clone.1 | convolution fusion | flops 2157444096 | bytes 6302212 | tf_op jit(solution)/shard_map/while/body/eval_jaxpr/dot_general | solution.py:67
  217.7 6.9 %fusion.56 = f32[1024]{0:T(1024)S(1)} fusion(bf16[1024,2048]{1,0:T(8,128)(2,1)} %get-tuple-element.168, bf16[8,512,2048]{2,1,0:T(8,128)(2,1)} %get-tuple-element.167, s32[]{:T(128)S(6)} %copy.19, s32[]{:T(128)} %get-tuple-element.171, s32[512]{0:T(512)S(1)} %add_multiply_fusion.2, s32[1024]{0:T(1024)S(1)} %fusion.55), kind=kOutput, calls=%fused_computation.21.clone.1 | convolution fusion | flops 2157444096 | bytes 6302212 | tf_op jit(solution)/shard_map/while/body/eval_jaxpr/dot_general | solution.py:67
  224.6 10.5 %pmax.7 = f32[1024]{0:T(1024)S(1)} all-reduce(f32[1024]{0:T(1024)S(1)} %get-tuple-element.45), channel_id=1, replica_groups=mesh['cent'=4,'rows'=32] {'cent'}, use_global_device_ids=true, to_apply=%region_3.4 | all-reduce | flops 1024 | bytes 8192 | tf_op jit(solution)/shard_map/pmax | solution.py:77
  235.1 0.6 dynamic_slice.11
  (51 shorter events, 7.9 us)
Async XLA Ops:
  7.2 94.6 %all-gather.5.cloned.1.call-start = ((), (), s32[]{:S(2)}) async-start(), calls=%async_computation.4 | async-start | bytes 5242880 | tf_op jit(solution)/shard_map/all_gather | solution.py:54
  7.9 150.9 %all-gather.3.cloned.1.call-start = ((), (), s32[]{:S(2)}) async-start(), calls=%async_computation.3 | async-start | bytes 17301504 | tf_op jit(solution)/shard_map/all_gather | solution.py:59
  13.2 20.4 %all-to-all-start = ((bf16[128,1,4]{2,1,0:T(2,128)(2,1)}), bf16[128,1,4]{2,1,0:T(2,128)(2,1)S(1)}, u32[]{:S(2)}, u32[]{:S(2)}) async-start(bf16[128,1,4]{2,1,0:T(2,128)(2,1)} %all_to_all.17), calls=%async_computation | async-start | bytes 131072 | tf_op jit(solution)/shard_map/all_to_all | solution.py:98
  33.6 39.2 %all-to-all-start.1 = ((bf16[128,4,2048]{2,1,0:T(4,128)(2,1)}), bf16[128,4,2048]{2,1,0:T(4,128)(2,1)S(1)}, u32[]{:S(2)}, u32[]{:S(2)}) async-start(bf16[128,4,2048]{2,1,0:T(4,128)(2,1)} %reshape.113), calls=%async_computation.1 | async-start | bytes 4194304 | tf_op jit(solution)/shard_map/all_to_all | solution.py:91
  81.5 16.3 %all-to-all-start.2 = ((f32[128,1,4]{2,1,0:T(1,128)}), f32[128,1,4]{2,1,0:T(1,128)S(1)}, u32[]{:S(2)}, u32[]{:S(2)}) async-start(f32[128,1,4]{2,1,0:T(1,128)} %bitcast.5), calls=%async_computation.2 | async-start | bytes 131072 | tf_op jit(solution)/shard_map/all_to_all | solution.py:109
Sparse Core Ops, SparseCore 0:
  9.7 73.9 all-gather.4
  85.9 72.9 all-gather.2
where the time goes:
time: 243 us
  waiting for transfers between devices  101 us (42%)
  matrix products  59 us (24%)
  starting transfers between devices  24.7 us (10%)
  local copies, waits for them, and re-layouts  20.6 us (8%)
  between operations  14.9 us (6%)
  blocking collectives  10.5 us (4%)
  other arithmetic  6.36 us (3%)
  loops' own time  5.28 us (2%)
    all_gather x1, waiting for transfers between devices, shards(): piece = lax.all_gather(centroids, 'rows', axis=0, tiled=True)  57.1 us
    dot_general x8, matrix products, step(): lax.dot_general(group, tile, (((1,), (1,)), ((), ())), preferred_element_...  55.4 us
    all_to_all x1, waiting for transfers between devices, shards(): lax.all_to_all(outgoing.reshape(devices, capacity, feature_dim), ('cent',...  32.1 us
    all_to_all x1, starting transfers between devices, shards(): lax.all_to_all(present.reshape(devices, capacity), ('cent', 'rows'), spli...  11.1 us
    pmax x1, blocking collectives, shards(): merged = lax.pmax(result, 'cent')  10.5 us
    all_to_all x1, waiting for transfers between devices, shards(): lax.all_to_all(scores.reshape(devices, capacity), ('cent', 'rows'), split...  7.23 us
    all_to_all x1, starting transfers between devices, shards(): lax.all_to_all(scores.reshape(devices, capacity), ('cent', 'rows'), split...  7.22 us
    all_to_all x1, starting transfers between devices, shards(): lax.all_to_all(outgoing.reshape(devices, capacity, feature_dim), ('cent',...  6.27 us
  transfers between devices with their start and end apart: 5, of which 4 were waited for; matrix products, arithmetic and copies ran while one was open for 10% of the time, Pallas kernels for 0%

commit v1 on v0

--- a/solution.py
+++ b/solution.py
@@ -56,7 +56,9 @@
     group_ids = (position // rows_dev * rows_count + rows_index) * rows_dev + position % rows_dev
     panel_base = cent_index * (rows_count * cent_dev)
     initial = jnp.full((cent_count * rows_dev,), -1e30, jnp.float32)
-    piece = lax.all_gather(centroids, "rows", axis=0, tiled=True)
+    low = jax.lax.psum(1, "rows")
+    field_out = jnp.concatenate(low * [centroids], 0)
+    piece = jax.lax.all_to_all(field_out, "rows", 0, 0, tiled=True)
     piece_rows = piece.shape[0]
     block = math.gcd(piece_rows, 512)
     tiles = piece.reshape(piece_rows // block, block, feature_dim)

time: 243 us -> 429 us (1.77)
  waiting for transfers between devices: 101 us -> 238 us
  local copies, waits for them, and re-layouts: 20.6 us -> 64.2 us
  starting transfers between devices: 24.7 us -> 30.9 us
    all_to_all x0 -> x1, waiting for transfers between devices: none -> 163 us  [shards(): piece = jax.lax.all_to_all(field_out, 'rows', 0, 0, tiled=True)]
    all_gather x1 -> x0, waiting for transfers between devices: 57.1 us -> none  [shards(): piece = lax.all_gather(centroids, 'rows', axis=0, tiled=True)]
    all_gather x1, waiting for transfers between devices: 0.01 us -> 43.5 us  [shards(): group = lax.all_gather(embeddings, 'cent', axis=0, tiled=True)]
    unnamed x0 -> x33, local copies, waits for them, and re-layouts: none -> 43 us
    all_to_all x1, waiting for transfers between devices: 32.1 us -> 22.8 us  [shards(): lax.all_to_all(outgoing.reshape(devices, capacity, feature_dim), ('cent',...]
    all_to_all x0 -> x1, starting transfers between devices: none -> 5.35 us  [shards(): piece = jax.lax.all_to_all(field_out, 'rows', 0, 0, tiled=True)]
  transfers between devices with their start and end apart: 5 -> 5, of which waited for: 4 -> 4; matrix products, arithmetic and copies ran while one was open for 10% -> 13% of each run, Pallas kernels for 0% -> 0%
where the time goes in v1:
time: 429 us; the launch traced here: 427 us
  waiting for transfers between devices  238 us (55%)
  local copies, waits for them, and re-layouts  64.2 us (15%)
  matrix products  59 us (14%)
  starting transfers between devices  30.9 us (7%)
  between operations  14.9 us (3%)
  blocking collectives  8.8 us (2%)
  other arithmetic  6.35 us (1%)
  loops' own time  4.89 us (1%)
    all_to_all x1, waiting for transfers between devices, shards(): piece = jax.lax.all_to_all(field_out, 'rows', 0, 0, tiled=True)  163 us
    dot_general x8, matrix products, step(): lax.dot_general(group, tile, (((1,), (1,)), ((), ())), preferred_element_...  55.4 us
    all_gather x1, waiting for transfers between devices, shards(): group = lax.all_gather(embeddings, 'cent', axis=0, tiled=True)  43.5 us
    unnamed x33, local copies, waits for them, and re-layouts  43 us
    all_to_all x1, waiting for transfers between devices, shards(): lax.all_to_all(outgoing.reshape(devices, capacity, feature_dim), ('cent',...  22.8 us
    all_to_all x1, starting transfers between devices, shards(): lax.all_to_all(present.reshape(devices, capacity), ('cent', 'rows'), spli...  11.1 us
    all_to_all x1, starting transfers between devices, shards(): lax.all_to_all(outgoing.reshape(devices, capacity, feature_dim), ('cent',...  9.76 us
    pmax x1, blocking collectives, shards(): merged = lax.pmax(result, 'cent')  8.8 us
  transfers between devices with their start and end apart: 5, of which 4 were waited for; matrix products, arithmetic and copies ran while one was open for 13% of the time, Pallas kernels for 0%

profile of v1, /device:TPU:0, one launch (start us, length us, event | category | flops | bytes accessed | tf_op | source)
XLA Modules:
  0.0 427.5 jit_solution(4961090898855214425)
XLA Ops:
  8.8 2.2 scatter_custom_fusion
  11.7 11.1 %all-to-all-start.1 = ((bf16[128,1,4]{2,1,0:T(2,128)(2,1)}), bf16[128,1,4]{2,1,0:T(2,128)(2,1)S(1)}, u32[]{:S(2)}, u32[]{:S(2)}) async-start(bf16[128,1,4]{2,1,0:T(2,128)(2,1)} %all_to_all.25), calls=%async_computation.1 | async-start | bytes 131072 | tf_op jit(solution)/shard_map/all_to_all | solution.py:100
  26.7 1.9 constant_dynamic-update-slice_fusion.29
  28.6 1.9 constant_dynamic-update-slice_fusion.28
  32.3 1.9 constant_dynamic-update-slice_fusion.26
  36.1 1.9 constant_dynamic-update-slice_fusion.24
  39.9 1.9 constant_dynamic-update-slice_fusion.22
  43.7 1.9 constant_dynamic-update-slice_fusion.20
  47.5 1.9 constant_dynamic-update-slice_fusion.18
  59.2 3.5 scatter_custom_fusion.1
  62.7 2.2 reshape.116
  64.9 9.8 %all-to-all-start.2 = ((bf16[128,4,2048]{2,1,0:T(4,128)(2,1)}), bf16[128,4,2048]{2,1,0:T(4,128)(2,1)S(1)}, u32[]{:S(2)}, u32[]{:S(2)}) async-start(bf16[128,4,2048]{2,1,0:T(4,128)(2,1)} %reshape.116), calls=%async_computation.2 | async-start | bytes 4194304 | tf_op jit(solution)/shard_map/all_to_all | solution.py:93
  82.2 22.8 %all-to-all-done.2 = bf16[128,4,2048]{2,1,0:T(4,128)(2,1)S(1)} async-done(((bf16[128,4,2048]{2,1,0:T(4,128)(2,1)}), bf16[128,4,2048]{2,1,0:T(4,128)(2,1)S(1)}, u32[]{:S(2)}, u32[]{:S(2)}) %all-to-all-start.2) | async-done | bytes 2097184 | tf_op jit(solution)/shard_map/all_to_all | solution.py:93
  105.1 2.1 fusion.33
  107.3 2.1 reshape.117
  109.4 3.6 fusion.37
  113.7 4.6 %all-to-all-start.3 = ((f32[128,1,4]{2,1,0:T(1,128)}), f32[128,1,4]{2,1,0:T(1,128)S(1)}, u32[]{:S(2)}, u32[]{:S(2)}) async-start(f32[128,1,4]{2,1,0:T(1,128)} %bitcast.6), calls=%async_computation.3 | async-start | bytes 131072 | tf_op jit(solution)/shard_map/all_to_all | solution.py:111
  119.2 8.5 %all-to-all-done.3 = f32[128,1,4]{2,1,0:T(1,128)S(1)} async-done(((f32[128,1,4]{2,1,0:T(1,128)}), f32[128,1,4]{2,1,0:T(1,128)S(1)}, u32[]{:S(2)}, u32[]{:S(2)}) %all-to-all-start.3) | async-done | bytes 2080 | tf_op jit(solution)/shard_map/all_to_all | solution.py:111
  127.7 5.3 %all-to-all-start = ((bf16[32,128,2048]{2,1,0:T(8,128)(2,1)}), bf16[32,128,2048]{2,1,0:T(8,128)(2,1)}, u32[]{:S(2)}, u32[]{:S(2)}) async-start(bf16[32,128,2048]{2,1,0:T(8,128)(2,1)} %bitcast), calls=%async_computation | async-start | bytes 33554432 | tf_op jit(solution)/shard_map/all_to_all | solution.py:61
  137.1 2.5 gather_fusion
  139.6 43.5 %all-gather.2.cloned.1.call-done = bf16[1024,2048]{1,0:T(8,128)(2,1)} async-done(((bf16[256,2048]{1,0:T(8,128)(2,1)}), bf16[1024,2048]{1,0:T(8,128)(2,1)}) %all-gather.2.cloned.1.call-update) | async-done | bytes 4194320 | tf_op jit(solution)/shard_map/all_gather | solution.py:54
  183.1 162.9 %all-to-all-done = bf16[32,128,2048]{2,1,0:T(8,128)(2,1)} async-done(((bf16[32,128,2048]{2,1,0:T(8,128)(2,1)}), bf16[32,128,2048]{2,1,0:T(8,128)(2,1)}, u32[]{:S(2)}, u32[]{:S(2)}) %all-to-all-start) | async-done | bytes 16777248 | tf_op jit(solution)/shard_map/all_to_all | solution.py:61
  346.1 65.1 %while.11 = (s32[]{:T(128)}, f32[1024]{0:T(1024)S(1)}, bf16[8,512,2048]{2,1,0:T(8,128)(2,1)}, bf16[1024,2048]{1,0:T(8,128)(2,1)}, s32[8]{0:T(128)S(1)}, /*index=...) while((s32[]{:T(128)}, f32[1024]{0:T(1024)S(1)}, bf16[8,512,2048]{2,1,0:T(8,128)(2,1)}, ...), condition=%wide.region_2.3_spmd.clone, body=%wide.region_0.2_spmd.clone.sunk | while | flops 2157464576 | bytes 6320795 | solution.py:78
  347.2 6.9 %fusion.56 = f32[1024]{0:T(1024)S(1)} fusion(bf16[1024,2048]{1,0:T(8,128)(2,1)} %get-tuple-element.168, bf16[8,512,2048]{2,1,0:T(8,128)(2,1)} %get-tuple-element.167, s32[]{:T(128)S(6)} %copy.50, s32[]{:T(128)} %get-tuple-element.171, s32[512]{0:T(512)S(1)} %add_multiply_fusion.2, s32[1024]{0:T(1024)S(1)} %fusion.55), kind=kOutput, calls=%fused_computation.21.clone.1 | convolution fusion | flops 2157444096 | bytes 6302212 | tf_op jit(solution)/shard_map/while/body/eval_jaxpr/dot_general | solution.py:69
  355.4 6.9 %fusion.56 = f32[1024]{0:T(1024)S(1)} fusion(bf16[1024,2048]{1,0:T(8,128)(2,1)} %get-tuple-element.168, bf16[8,512,2048]{2,1,0:T(8,128)(2,1)} %get-tuple-element.167, s32[]{:T(128)S(6)} %copy.50, s32[]{:T(128)} %get-tuple-element.171, s32[512]{0:T(512)S(1)} %add_multiply_fusion.2, s32[1024]{0:T(1024)S(1)} %fusion.55), kind=kOutput, calls=%fused_computation.21.clone.1 | convolution fusion | flops 2157444096 | bytes 6302212 | tf_op jit(solution)/shard_map/while/body/eval_jaxpr/dot_general | solution.py:69
  363.5 6.9 %fusion.56 = f32[1024]{0:T(1024)S(1)} fusion(bf16[1024,2048]{1,0:T(8,128)(2,1)} %get-tuple-element.168, bf16[8,512,2048]{2,1,0:T(8,128)(2,1)} %get-tuple-element.167, s32[]{:T(128)S(6)} %copy.50, s32[]{:T(128)} %get-tuple-element.171, s32[512]{0:T(512)S(1)} %add_multiply_fusion.2, s32[1024]{0:T(1024)S(1)} %fusion.55), kind=kOutput, calls=%fused_computation.21.clone.1 | convolution fusion | flops 2157444096 | bytes 6302212 | tf_op jit(solution)/shard_map/while/body/eval_jaxpr/dot_general | solution.py:69
  371.7 6.9 %fusion.56 = f32[1024]{0:T(1024)S(1)} fusion(bf16[1024,2048]{1,0:T(8,128)(2,1)} %get-tuple-element.168, bf16[8,512,2048]{2,1,0:T(8,128)(2,1)} %get-tuple-element.167, s32[]{:T(128)S(6)} %copy.50, s32[]{:T(128)} %get-tuple-element.171, s32[512]{0:T(512)S(1)} %add_multiply_fusion.2, s32[1024]{0:T(1024)S(1)} %fusion.55), kind=kOutput, calls=%fused_computation.21.clone.1 | convolution fusion | flops 2157444096 | bytes 6302212 | tf_op jit(solution)/shard_map/while/body/eval_jaxpr/dot_general | solution.py:69
  379.8 6.9 %fusion.56 = f32[1024]{0:T(1024)S(1)} fusion(bf16[1024,2048]{1,0:T(8,128)(2,1)} %get-tuple-element.168, bf16[8,512,2048]{2,1,0:T(8,128)(2,1)} %get-tuple-element.167, s32[]{:T(128)S(6)} %copy.50, s32[]{:T(128)} %get-tuple-element.171, s32[512]{0:T(512)S(1)} %add_multiply_fusion.2, s32[1024]{0:T(1024)S(1)} %fusion.55), kind=kOutput, calls=%fused_computation.21.clone.1 | convolution fusion | flops 2157444096 | bytes 6302212 | tf_op jit(solution)/shard_map/while/body/eval_jaxpr/dot_general | solution.py:69
  387.9 6.9 %fusion.56 = f32[1024]{0:T(1024)S(1)} fusion(bf16[1024,2048]{1,0:T(8,128)(2,1)} %get-tuple-element.168, bf16[8,512,2048]{2,1,0:T(8,128)(2,1)} %get-tuple-element.167, s32[]{:T(128)S(6)} %copy.50, s32[]{:T(128)} %get-tuple-element.171, s32[512]{0:T(512)S(1)} %add_multiply_fusion.2, s32[1024]{0:T(1024)S(1)} %fusion.55), kind=kOutput, calls=%fused_computation.21.clone.1 | convolution fusion | flops 2157444096 | bytes 6302212 | tf_op jit(solution)/shard_map/while/body/eval_jaxpr/dot_general | solution.py:69
  396.1 6.9 %fusion.56 = f32[1024]{0:T(1024)S(1)} fusion(bf16[1024,2048]{1,0:T(8,128)(2,1)} %get-tuple-element.168, bf16[8,512,2048]{2,1,0:T(8,128)(2,1)} %get-tuple-element.167, s32[]{:T(128)S(6)} %copy.50, s32[]{:T(128)} %get-tuple-element.171, s32[512]{0:T(512)S(1)} %add_multiply_fusion.2, s32[1024]{0:T(1024)S(1)} %fusion.55), kind=kOutput, calls=%fused_computation.21.clone.1 | convolution fusion | flops 2157444096 | bytes 6302212 | tf_op jit(solution)/shard_map/while/body/eval_jaxpr/dot_general | solution.py:69
  404.2 6.9 %fusion.56 = f32[1024]{0:T(1024)S(1)} fusion(bf16[1024,2048]{1,0:T(8,128)(2,1)} %get-tuple-element.168, bf16[8,512,2048]{2,1,0:T(8,128)(2,1)} %get-tuple-element.167, s32[]{:T(128)S(6)} %copy.50, s32[]{:T(128)} %get-tuple-element.171, s32[512]{0:T(512)S(1)} %add_multiply_fusion.2, s32[1024]{0:T(1024)S(1)} %fusion.55), kind=kOutput, calls=%fused_computation.21.clone.1 | convolution fusion | flops 2157444096 | bytes 6302212 | tf_op jit(solution)/shard_map/while/body/eval_jaxpr/dot_general | solution.py:69
  411.2 8.8 %pmax.7 = f32[1024]{0:T(1024)S(1)} all-reduce(f32[1024]{0:T(1024)S(1)} %get-tuple-element.45), channel_id=1, replica_groups=mesh['cent'=4,'rows'=32] {'cent'}, use_global_device_ids=true, to_apply=%region_3.4 | all-reduce | flops 1024 | bytes 8192 | tf_op jit(solution)/shard_map/pmax | solution.py:79
  (84 shorter events, 43.4 us)
Async XLA Ops:
  7.2 46.0 %copy-start = (bf16[128,2048]{1,0:T(8,128)(2,1)S(1)}, bf16[128,2048]{1,0:T(8,128)(2,1)}, u32[]{:S(2)}) copy-start(bf16[128,2048]{1,0:T(8,128)(2,1)} %param.7) | copy-start | bytes 1572868
  11.7 53.2 %all-to-all-start.1 = ((bf16[128,1,4]{2,1,0:T(2,128)(2,1)}), bf16[128,1,4]{2,1,0:T(2,128)(2,1)S(1)}, u32[]{:S(2)}, u32[]{:S(2)}) async-start(bf16[128,1,4]{2,1,0:T(2,128)(2,1)} %all_to_all.25), calls=%async_computation.1 | async-start | bytes 131072 | tf_op jit(solution)/shard_map/all_to_all | solution.py:100
  64.9 40.2 %all-to-all-start.2 = ((bf16[128,4,2048]{2,1,0:T(4,128)(2,1)}), bf16[128,4,2048]{2,1,0:T(4,128)(2,1)S(1)}, u32[]{:S(2)}, u32[]{:S(2)}) async-start(bf16[128,4,2048]{2,1,0:T(4,128)(2,1)} %reshape.116), calls=%async_computation.2 | async-start | bytes 4194304 | tf_op jit(solution)/shard_map/all_to_all | solution.py:93
  113.7 13.9 %all-to-all-start.3 = ((f32[128,1,4]{2,1,0:T(1,128)}), f32[128,1,4]{2,1,0:T(1,128)S(1)}, u32[]{:S(2)}, u32[]{:S(2)}) async-start(f32[128,1,4]{2,1,0:T(1,128)} %bitcast.6), calls=%async_computation.3 | async-start | bytes 131072 | tf_op jit(solution)/shard_map/all_to_all | solution.py:111
  127.7 218.4 %all-to-all-start = ((bf16[32,128,2048]{2,1,0:T(8,128)(2,1)}), bf16[32,128,2048]{2,1,0:T(8,128)(2,1)}, u32[]{:S(2)}, u32[]{:S(2)}) async-start(bf16[32,128,2048]{2,1,0:T(8,128)(2,1)} %bitcast), calls=%async_computation | async-start | bytes 33554432 | tf_op jit(solution)/shard_map/all_to_all | solution.py:61
  133.0 50.1 %all-gather.2.cloned.1.call-start = ((), (), s32[]{:S(2)}) async-start(), calls=%async_computation.4 | async-start | bytes 5242880 | tf_op jit(solution)/shard_map/all_gather | solution.py:54
Sparse Core Ops, SparseCore 0:
  135.5 47.5 all-gather.1
